TPU v7x, 128 devices: a whole 4x4x4 slice. The times are simulated.
128 devices in a mesh: segment: 4 (over z), exp: 32 (over y, x, core).
Axes of the slice: x: 4, y: 4, z: 4, core: 2. Of those that a mesh axis runs over, the one named last changes fastest.
Arguments:
- hidden_rows: bfloat16 [16384, 2048], P(('segment', 'exp')), may hold values from -60 to 60, as said below
- norm_gain: float32 [2048], replicated, may hold values from 0.5 to 1.5
- router_weight: bfloat16 [2048, 64], replicated, may hold values from -0.25 to 0.25
- expert_ids: int32 [16384, 6], P(('segment', 'exp')), may hold values from 0 to 63, all different within a row; in each aligned block of 64 rows (0 to 63, 64 to 127, ...) at most 7 rows name the same one
- gate_weight: bfloat16 [4, 32, 704, 2048], P('segment', 'exp'), may hold values from -0.125 to 0.125
- up_weight: bfloat16 [4, 32, 704, 2048], P('segment', 'exp'), may hold values from -0.125 to 0.125
- down_weight: bfloat16 [4, 32, 704, 2048], P('segment', 'exp'), may hold values from -0.15625 to 0.15625
- latent_gain: float32 [2048], replicated, may hold values from 0.5 to 1.5
- kv_weight: bfloat16 [2048, 512], replicated, may hold values from -0.125 to 0.125
Outputs:
- expert_mix: bfloat16 [16384, 2048], P(('segment', 'exp'))
- latents: bfloat16 [16384, 512], P(('segment', 'exp'))
- gram_input: float32 [4, 32, 1024, 2048], P('segment', 'exp')
- gram_hidden: float32 [4, 32, 704, 1408], P('segment', 'exp')
Inputs may be any that keep to these rules, and one draw needn't show every extreme that they name: `expert_ids`: each row names 6 different experts and every expert is named somewhere. In each aligned block of 64 rows (one micro-batch of one device) no expert is named more than 7 times, and in some blocks some expert is named exactly 7 times. `hidden_rows`: activations of the attention section.
All inputs are finite; a program needn't handle non-finite values.
Results may differ from a plain program's by a relative error of at most 0.0068.
Values may be sent and summed in bfloat16 or wider, within the bound.
No kernel may reach another device: no remote copies, remote signals or barrier semaphores. Data moves between devices by JAX's collectives and lax.ppermute only.
A program may use at most 192 MiB of HBM per device.

v0:
```python
import functools

import jax
import jax.numpy as jnp
from jax import lax
from jax.experimental import pallas as pl
from jax.experimental.pallas import tpu as pltpu
from jax.sharding import PartitionSpec as P


MB_TOK = 64
MATE, FAR, OUTER = 1, 2, 3
SIZES = (24, 16, 16)
RETURNS = ((0, 1), (2,))
F32 = jnp.float32
BF16 = jnp.bfloat16


def swapped(value, mask):
    pairs = [(source, source ^ mask) for source in range(lax.axis_size("segment"))]
    return lax.ppermute(value, "segment", pairs)


def rms_norm(values, gain):
    mean_square = jnp.mean(values * values, axis=-1, keepdims=True)
    return values * lax.rsqrt(mean_square + 1e-06) * gain


def exchanged(value):
    return lax.all_to_all(value, "exp", split_axis=0, concat_axis=0, tiled=True)


def dot(left, right, dims):
    return lax.dot_general(left, right, (dims, ((), ())), preferred_element_type=F32)


def layer(
    hidden_rows,
    norm_gain,
    router_weight,
    expert_ids,
    gate_weight,
    up_weight,
    down_weight,
    latent_gain,
    kv_weight,
):
    columns = lax.axis_size("exp")
    model_width = hidden_rows.shape[1]
    width_half = model_width // 2
    experts = router_weight.shape[1]
    top_count = expert_ids.shape[1]
    rows = hidden_rows.shape[0]
    capacity = MB_TOK * top_count * 5 // (4 * experts)
    segment = lax.axis_index("segment")
    half = segment % 2
    pair = segment // 2
    w_gate = gate_weight[0, 0]
    w_up = up_weight[0, 0]
    w_down = down_weight[0, 0]

    residual = hidden_rows.astype(F32)
    normed = rms_norm(residual, norm_gain).astype(BF16)
    normed, ids_t = lax.optimization_barrier((normed, expert_ids.T))
    ids_mate = swapped(ids_t, MATE)
    rows_mate = swapped(normed, MATE)
    rows_outer = swapped(normed, OUTER)
    ids_outer = swapped(ids_t, OUTER)
    ids_far = swapped(ids_t, FAR)
    mid = rows // 2
    far_low = swapped(rows_outer[:mid], MATE)
    far_high = swapped(rows_mate[mid:], OUTER)
    tokens_pair = jnp.concatenate([normed, rows_mate], axis=0)
    tokens_far = jnp.concatenate([rows_outer, far_low, far_high], axis=0)
    tokens_all = jnp.concatenate([tokens_pair, tokens_far], axis=0)

    own_cols = lax.dynamic_slice_in_dim(w_down, half * width_half, width_half, 1)
    other_cols = lax.dynamic_slice_in_dim(w_down, (1 - half) * width_half, width_half, 1)
    other_cols, far_low, far_high = lax.optimization_barrier((other_cols, far_low, far_high))
    partner_cols = swapped(other_cols, MATE)
    first = half == 0
    down_cols = jnp.concatenate(
        [jnp.where(first, own_cols, partner_cols), jnp.where(first, partner_cols, own_cols)],
        axis=0,
    )

    expert_grid = jnp.arange(experts, dtype=jnp.int32)
    own_grid = expert_grid[:columns] + pair * columns
    block = jnp.arange(rows, dtype=jnp.int32)
    earlier = (block[:, None] < block[None, :]) & (
        block[:, None] // MB_TOK == block[None, :] // MB_TOK
    )
    earlier = earlier.astype(BF16)

    def slots_of(ids, position):
        chosen = jnp.any(ids[:, None, :] == own_grid[None, :, None], axis=0)
        rank = dot(chosen.astype(BF16), earlier, ((1,), (0,))).astype(jnp.int32)
        base = capacity * (block // MB_TOK + position * (rows // MB_TOK))
        return jnp.where(chosen, rank + base[None, :], -1)

    slot_pair = jnp.concatenate([slots_of(ids_t, half), slots_of(ids_mate, 1 - half)], axis=1)
    slot_late, ids_outer, ids_far = lax.optimization_barrier((slot_pair, ids_outer, ids_far))
    slot_far = jnp.concatenate([slots_of(ids_outer, 3 - half), slots_of(ids_far, 2 + half)], axis=1)
    slot_all = jnp.concatenate([slot_late, slot_far], axis=1)
    ids_all = jnp.concatenate([ids_t, ids_mate, ids_outer, ids_far], axis=1)

    def hits(slot, low, size):
        grid = low + jnp.arange(size, dtype=jnp.int32)
        return slot[:, None, :] == grid[None, :, None]

    chosen = jnp.any(ids_all[:, None, :] == expert_grid[None, :, None], axis=0)
    logits_t = dot(router_weight, tokens_all, ((0,), (1,)))
    affinity = jnp.where(chosen, jax.nn.sigmoid(logits_t), 0.0)
    share_all = affinity / jnp.sum(affinity, axis=0, keepdims=True)
    share = lax.dynamic_slice_in_dim(share_all, pair * columns, columns, 0)

    lows = [sum(SIZES[:i]) for i in range(len(SIZES))]
    sides = ((slot_pair, tokens_pair), (slot_all, tokens_all), (slot_far, tokens_far))
    counts = jnp.sum((slot_all >= 0).astype(F32), axis=1)
    last = len(SIZES) - 1
    received = []
    count_total = None
    for index, (low, size) in enumerate(zip(lows, SIZES)):
        slot, tokens = sides[index]
        picks = hits(slot, low, size).astype(BF16).reshape(columns * size, slot.shape[1])
        buffer = dot(picks, tokens, ((1,), (0,))).astype(BF16)
        buffer = buffer.reshape(columns, size, model_width)
        if index == last:
            extra = jnp.broadcast_to(counts.astype(BF16)[:, None, None], (columns, size, 128))
            buffer = jnp.concatenate([buffer, extra], axis=2)
        if index == last:
            arrived = exchanged(buffer)
            count_total = jnp.sum(arrived[:, 0, model_width].astype(F32))
            arrived = arrived[:, :, :model_width]
        else:
            arrived = exchanged(buffer)
        received.append(arrived.reshape(columns * size, model_width))
    hidden, full, outs = [], [], []
    for value in received:
        gate_pre = dot(w_gate, value, ((1,), (1,)))
        up_pre = dot(w_up, value, ((1,), (1,)))
        own_t = (jax.nn.silu(gate_pre) * up_pre).astype(BF16)
        other_t = swapped(own_t, MATE)
        full_t = jnp.concatenate(
            [jnp.where(first, own_t, other_t), jnp.where(first, other_t, own_t)], axis=0
        )
        out = dot(full_t, down_cols, ((0,), (0,))).astype(BF16)
        hidden.append(own_t)
        full.append(full_t)
        outs.append(out.reshape(columns, -1, width_half))

    mixes = []
    for group, slot, part in ((RETURNS[0], slot_all, share), (RETURNS[1], slot_far, share[:, 2 * rows :])):
        low, size = lows[group[0]], sum(SIZES[i] for i in group)
        sent = jnp.concatenate([outs[i] for i in group], axis=1)
        back = exchanged(sent)
        back = back.reshape(columns * size, width_half)
        table = jnp.where(hits(slot, low, size), part[:, None, :], 0.0)
        table = table.reshape(columns * size, slot.shape[1])
        mixes.append(dot(table.astype(BF16), back, ((0,), (0,))))
    mix_own = mixes[0][:rows]
    mix_mate = mixes[0][rows : 2 * rows]
    mix_far = mixes[0][2 * rows :] + mixes[1]
    from_far = swapped(mix_far[rows:].astype(BF16), FAR)
    from_outer = swapped(mix_far[:rows].astype(BF16), OUTER)
    from_mate = swapped(mix_mate.astype(BF16), MATE)
    mine = mix_own + from_far.astype(F32)
    others = from_mate.astype(F32) + from_outer.astype(F32)
    expert_mix = jnp.concatenate(
        [jnp.where(first, mine, others), jnp.where(first, others, mine)], axis=1
    ).astype(BF16)
    combined = residual + expert_mix.astype(F32)
    normed_next = rms_norm(combined, latent_gain).astype(BF16)
    latents = jnp.dot(normed_next, kv_weight, preferred_element_type=F32).astype(BF16)

    inverse_count = 2.0 / count_total
    gram_first = hidden_gram(hidden[:1], full[:1])
    gram_hid = hidden_gram(hidden[1:], full[1:], gram_first, inverse_count)
    gram_in = scaled_gram(half, inverse_count, received, width_half)
    return (expert_mix, latents, gram_in[None, None], gram_hid[None, None])


def gram_kernel(half_ref, scale_ref, *refs):
    count = len(SIZES)
    left, right, out_ref, turned = refs[:count], refs[count : 2 * count], refs[-2], refs[-1]
    ends = [0]
    for ref in left:
        ends.append(ends[-1] + ref.shape[0])

    @pl.when(pl.program_id(1) == 0)
    def _():
        for ref, low, high in zip(left, ends, ends[1:]):
            turned[:, low:high] = ref[...].T

    total = None
    for ref, low, high in zip(right, ends, ends[1:]):
        part = dot(turned[:, low:high], ref[...], ((1,), (0,)))
        total = part if total is None else total + part
    out_ref[...] = total * scale_ref[0, 0]


def scaled_gram(half, scale, chunks, out_rows):
    width = chunks[0].shape[1]
    tile, wide = 512, 512
    steps = out_rows // tile
    left = [
        pl.BlockSpec((c.shape[0], tile), lambda i, j, half: (0, half[0] * steps + i)) for c in chunks
    ]
    right = [pl.BlockSpec((c.shape[0], wide), lambda i, j, half: (0, j)) for c in chunks]
    depth = sum(c.shape[0] for c in chunks)
    return pl.pallas_call(
        gram_kernel,
        grid_spec=pltpu.PrefetchScalarGridSpec(
            num_scalar_prefetch=1,
            grid=(steps, width // wide),
            in_specs=[pl.BlockSpec(memory_space=pltpu.SMEM), *left, *right],
            out_specs=pl.BlockSpec((tile, wide), lambda i, j, half: (i, j)),
            scratch_shapes=[pltpu.VMEM((tile, depth), BF16)],
        ),
        out_shape=jax.ShapeDtypeStruct((out_rows, width), F32),
        cost_estimate=pl.CostEstimate(
            flops=2 * depth * out_rows * width,
            transcendentals=0,
            bytes_accessed=4 * out_rows * width + 6 * depth * width,
        ),
    )(half.astype(jnp.int32).reshape(1), scale.reshape(1, 1), *chunks, *chunks)


def hidden_gram_kernel(count, *refs):
    own, full = refs[:count], refs[count : 2 * count]
    total = None
    for a_ref, b_ref in zip(own, full):
        part = dot(a_ref[...], b_ref[...], ((1,), (1,)))
        total = part if total is None else total + part
    if len(refs) > 2 * count + 1:
        base_ref, scale_ref = refs[2 * count : 2 * count + 2]
        total = (total + base_ref[...]) * scale_ref[0, 0]
    refs[-1][...] = total


def hidden_gram(own, full, base=None, scale=None):
    units, width = own[0].shape[0], full[0].shape[0]
    tile = 128
    depth = sum(v.shape[1] for v in own)
    out_spec = pl.BlockSpec((units, tile), lambda j: (0, j))
    operands = (*own, *full)
    specs = [
        *[pl.BlockSpec((units, v.shape[1]), lambda j: (0, 0)) for v in own],
        *[pl.BlockSpec((tile, v.shape[1]), lambda j: (j, 0)) for v in full],
    ]
    if base is not None:
        operands += (base, scale.reshape(1, 1))
        specs += [out_spec, pl.BlockSpec(memory_space=pltpu.SMEM)]
    return pl.pallas_call(
        functools.partial(hidden_gram_kernel, len(own)),
        grid=(width // tile,),
        in_specs=specs,
        out_specs=out_spec,
        out_shape=jax.ShapeDtypeStruct((units, width), F32),
        cost_estimate=pl.CostEstimate(
            flops=2 * depth * units * width,
            transcendentals=0,
            bytes_accessed=4 * units * width + 2 * depth * (units + width),
        ),
    )(*operands)


def solution(mesh):
    return jax.shard_map(
        layer,
        mesh=mesh,
        in_specs=(
            P(("segment", "exp"), None),
            P(),
            P(),
            P(("segment", "exp"), None),
            P("segment", "exp", None, None),
            P("segment", "exp", None, None),
            P("segment", "exp", None, None),
            P(),
            P(),
        ),
        out_specs=(
            P(("segment", "exp"), None),
            P(("segment", "exp"), None),
            P("segment", "exp", None, None),
            P("segment", "exp", None, None),
        ),
        check_vma=False,
    )
```

profile of v0, /device:TPU:26, one launch (start us, length us, event | category | flops | bytes accessed | tf_op | source)
XLA Modules:
  0.0 305.7 jit_solution(12524364124891770849)
XLA Ops:
  0.7 1.4 fusion.60
  3.3 4.1 %collective-permute-start.4 = (bf16[128,2048]{1,0:T(8,128)(2,1)S(1)}, bf16[128,2048]{1,0:T(8,128)(2,1)}, u32[]{:S(2)}, u32[]{:S(2)}) collective-permute-start(bf16[128,2048]{1,0:T(8,128)(2,1)S(1)} %fusion.62), channel_id=1, source_target_pairs={{0,96},{32,64},{64,32},{96,0},{1,97},{33,65},{65,33},{97,1},{2,98}... | collective-permute-start | bytes 1572872 | tf_op jit(solution)/shard_map/ppermute | solution.py:21
  7.4 2.0 collective-permute-start
  9.5 2.0 collective-permute-start.2
  12.5 8.5 %collective-permute-done = s32[6,128]{1,0:T(8,128)S(1)} collective-permute-done((s32[6,128]{1,0:T(8,128)}, s32[6,128]{1,0:T(8,128)S(1)}, u32[]{:S(2)}, u32[]{:S(2)}) %collective-permute-start) | collective-permute-done | bytes 3104 | tf_op jit(solution)/shard_map/ppermute | solution.py:21
  25.2 1.6 collective-permute-start.6
  26.8 1.9 constant_dynamic-update-slice_fusion.3
  28.7 1.9 constant_dynamic-update-slice_fusion.2
  34.8 4.2 %convolution_convert_fusion.2 = bf16[512,2048]{1,0:T(8,128)(2,1)} fusion(pred[512,512]{1,0:T(32,128)(4,1)S(1)} %bitcast_compare_fusion, bf16[512,2048]{1,0:T(8,128)(2,1)} %constant_dynamic-update-slice_fusion), kind=kOutput, calls=%fused_computation.2 | convolution fusion | flops 1074790400 | bytes 4456448 | tf_op jit(solution)/shard_map/dot_general | solution.py:34
  38.9 7.4 %all-to-all-start.1 = ((bf16[32,16,2048]{2,1,0:T(8,128)(2,1)}), bf16[32,16,2048]{2,1,0:T(8,128)(2,1)}, u32[]{:S(2)}, u32[]{:S(2)}) async-start(bf16[32,16,2048]{2,1,0:T(8,128)(2,1)} %bitcast.127), calls=%async_computation.1 | async-start | bytes 4194304 | tf_op jit(solution)/shard_map/all_to_all | solution.py:30
  48.5 1.9 convolution_convert_fusion.1
  50.5 1.5 pad_maximum_fusion.2
  52.1 20.0 %all-to-all-done.1 = bf16[32,16,2048]{2,1,0:T(8,128)(2,1)} async-done(((bf16[32,16,2048]{2,1,0:T(8,128)(2,1)}), bf16[32,16,2048]{2,1,0:T(8,128)(2,1)}, u32[]{:S(2)}, u32[]{:S(2)}) %all-to-all-start.1) | async-done | bytes 2097184 | tf_op jit(solution)/shard_map/all_to_all | solution.py:30
  72.1 9.1 %all-to-all-start.3 = ((bf16[32,16,2176]{2,1,0:T(8,128)(2,1)}), bf16[32,16,2176]{2,1,0:T(8,128)(2,1)}, u32[]{:S(2)}, u32[]{:S(2)}) async-start(bf16[32,16,2176]{2,1,0:T(8,128)(2,1)} %pad_maximum_fusion.2), calls=%async_computation.3 | async-start | bytes 4456448 | tf_op jit(solution)/shard_map/all_to_all | solution.py:30
  81.5 3.7 %convolution_convert_fusion = bf16[768,2048]{1,0:T(8,128)(2,1)} fusion(pred[768,256]{1,0:T(32,128)(4,1)S(1)} %bitcast_compare_fusion.1, bf16[128,2048]{1,0:T(8,128)(2,1)} %collective-permute-done.3, bf16[128,2048]{1,0:T(8,128)(2,1)S(1)} %fusion.62), kind=kOutput, calls=%fused_computation | convolution fusion | flops 808976384 | bytes 4390912 | tf_op jit(solution)/shard_map/dot_general | solution.py:34
  85.2 23.1 %all-to-all-done.3 = bf16[32,16,2176]{2,1,0:T(8,128)(2,1)} async-done(((bf16[32,16,2176]{2,1,0:T(8,128)(2,1)}), bf16[32,16,2176]{2,1,0:T(8,128)(2,1)}, u32[]{:S(2)}, u32[]{:S(2)}) %all-to-all-start.3) | async-done | bytes 2228256 | tf_op jit(solution)/shard_map/all_to_all | solution.py:30
  108.3 9.3 %all-to-all-start = ((bf16[32,24,2048]{2,1,0:T(8,128)(2,1)}), bf16[32,24,2048]{2,1,0:T(8,128)(2,1)}, u32[]{:S(2)}, u32[]{:S(2)}) async-start(bf16[32,24,2048]{2,1,0:T(8,128)(2,1)} %bitcast.121), calls=%async_computation | async-start | bytes 6291456 | tf_op jit(solution)/shard_map/all_to_all | solution.py:30
  117.6 2.6 dynamic-slice_bitcast_fusion
  120.7 2.5 fusion.92
  123.3 30.9 %collective-permute-done.8 = bf16[704,1024]{1,0:T(8,128)(2,1)} collective-permute-done((bf16[704,1024]{1,0:T(8,128)(2,1)}, bf16[704,1024]{1,0:T(8,128)(2,1)}, u32[]{:S(2)}, u32[]{:S(2)}) %collective-permute-start.8) | collective-permute-done | bytes 1441824 | tf_op jit(solution)/shard_map/ppermute | solution.py:21
  154.2 3.8 %bitcast_select_fusion.1 = (bf16[704,1024]{1,0:T(8,128)(2,1)}, bf16[704,1024]{1,0:T(8,128)(2,1)}) fusion(bf16[704,1024]{1,0:T(8,128)(2,1)} %collective-permute-done.8, pred[]{:T(512)S(6)} %eq.183, bf16[1,1,704,2048]{3,2,1,0:T(8,128)(2,1)S(1)} %copy-done.4, s32[]{:T(128)S(6)} %select_n.170), kind=kLoop, calls=%fused_computation.44 | loop fusion | flops 1441792 | bytes 5767173 | tf_op jit(solution)/shard_map/jit(_where)/select_n | solution.py:83
  158.0 3.4 %fusion.18 = f32[704,512]{1,0:T(8,128)S(1)} fusion(bf16[512,2048]{1,0:T(8,128)(2,1)} %bitcast.14.refs_1_.refs_4_, bf16[1,1,704,2048]{3,2,1,0:T(8,128)(2,1)S(1)} %copy-done), kind=kOutput, calls=%fused_computation.35 | convolution fusion | flops 1476395008 | bytes 6422528 | tf_op jit(solution)/shard_map/dot_general | solution.py:34
  161.4 4.3 %fusion.39.refs_0_ = bf16[704,512]{1,0:T(8,128)(2,1)} fusion(bf16[512,2048]{1,0:T(8,128)(2,1)} %bitcast.14.refs_1_.refs_4_, bf16[1,1,704,2048]{3,2,1,0:T(8,128)(2,1)S(1)} %copy-done.28, f32[704,512]{1,0:T(8,128)S(1)} %fusion.18), kind=kOutput, calls=%fused_computation.47 | convolution fusion | flops 1478557696 | bytes 7143424 | tf_op jit(solution)/shard_map/dot_general | solution.py:34
  166.0 3.2 %slice.52 = bf16[32,16,2048]{2,1,0:T(8,128)(2,1)} slice(bf16[32,16,2176]{2,1,0:T(8,128)(2,1)} %all-to-all-done.3), slice={[0:32], [0:16], [0:2048]} | slice | bytes 4194304 | tf_op jit(solution)/shard_map/slice | solution.py:134
  169.2 4.5 %fusion.10 = f32[768,704]{0,1:T(8,128)S(1)} fusion(bf16[768,2048]{1,0:T(8,128)(2,1)} %bitcast.4.refs_0_.refs_3_, bf16[1,1,704,2048]{3,2,1,0:T(8,128)(2,1)S(1)} %copy-done), kind=kOutput, calls=%fused_computation.14 | convolution fusion | flops 2214592512 | bytes 8192000 | tf_op jit(solution)/shard_map/dot_general | solution.py:34
  173.7 4.7 %fusion.12.refs_0_ = bf16[704,768]{1,0:T(8,128)(2,1)S(1)} fusion(f32[768,704]{0,1:T(8,128)S(1)} %fusion.10, bf16[768,2048]{1,0:T(8,128)(2,1)} %bitcast.4.refs_0_.refs_3_, bf16[1,1,704,2048]{3,2,1,0:T(8,128)(2,1)S(1)} %copy-done.29), kind=kOutput, calls=%fused_computation.22 | convolution fusion | flops 2217836544 | bytes 9273344 | tf_op jit(solution)/shard_map/dot_general | solution.py:34
  178.5 2.1 collective-permute-start.7
  180.5 2.8 fusion.21
  183.3 1.8 collective-permute-done.9
  185.1 1.4 broadcast_select_fusion.5
  186.5 1.8 convolution_convert_fusion.5
  188.4 18.1 %collective-permute-done.7 = bf16[704,768]{1,0:T(8,128)(2,1)S(1)} collective-permute-done((bf16[704,768]{1,0:T(8,128)(2,1)S(1)}, bf16[704,768]{1,0:T(8,128)(2,1)S(1)}, u32[]{:S(2)}, u32[]{:S(2)}) %collective-permute-start.7) | collective-permute-done | bytes 1081376 | tf_op jit(solution)/shard_map/ppermute | solution.py:21
  206.6 2.6 convolution_convert_fusion.3
  209.2 1.8 pad_maximum_fusion.1
  211.0 7.4 %all-to-all-start.2 = ((bf16[32,40,1024]{2,1,0:T(8,128)(2,1)}), bf16[32,40,1024]{2,1,0:T(8,128)(2,1)}, u32[]{:S(2)}, u32[]{:S(2)}) async-start(bf16[32,40,1024]{2,1,0:T(8,128)(2,1)} %pad_maximum_fusion.1), calls=%async_computation.2 | async-start | bytes 5242880 | tf_op jit(solution)/shard_map/all_to_all | solution.py:30
  218.5 4.7 %fusion.36.refs_1_ = bf16[704,512]{1,0:T(8,128)(2,1)S(1)} fusion(bf16[512,2048]{1,0:T(8,128)(2,1)} %bitcast.123, bf16[1,1,704,2048]{3,2,1,0:T(8,128)(2,1)} %param.14, f32[704,512]{1,0:T(8,128)} %fusion.21), kind=kOutput, calls=%fused_computation.46 | convolution fusion | flops 1478557696 | bytes 7143424 | tf_op jit(solution)/shard_map/dot_general | solution.py:34
  223.6 1.5 fusion.83
  225.7 2.5 pad_maximum_fusion.4.refs_2_
  228.3 16.4 %shard_map.120 = f32[1024,2048]{1,0:T(8,128)} custom-call(s32[1]{0:T(128)} %bitcast.26.half_ref, f32[1,1]{1,0:T(1,128)} %bitcast.27.scale_ref.refs_5_, bf16[768,2048]{1,0:T(8,128)(2,1)} %bitcast.4.refs_0_.refs_3_, bf16[512,2048]{1,0:T(8,128)(2,1)} %bitcast.14.refs_1_.refs_4_, bf16[512,2048]{1,0:T(8,128)(2,1)} %bitcast.124, ...), custom_call_target="tpu_custom_call" | custom-call | flops 7516192768 | bytes 30408704 | tf_op jit(solution)/shard_map/pallas_call | solution.py:211
  248.2 2.8 convolution_convert_fusion.4
  251.0 8.3 %all-to-all-start.4 = ((bf16[32,16,1024]{2,1,0:T(8,128)(2,1)}), bf16[32,16,1024]{2,1,0:T(8,128)(2,1)}, u32[]{:S(2)}, u32[]{:S(2)}) async-start(bf16[32,16,1024]{2,1,0:T(8,128)(2,1)} %bitcast.131), calls=%async_computation.4 | async-start | bytes 2097152 | tf_op jit(solution)/shard_map/all_to_all | solution.py:30
  259.3 1.5 pad_maximum_fusion.3.refs_1_
  260.8 3.3 %convolution_bitcast_fusion = f32[512,1024]{1,0:T(8,128)S(1)} fusion(bf16[32,40,1024]{2,1,0:T(8,128)(2,1)} %all-to-all-done.2, bf16[32,512]{1,0:T(8,128)(2,1)S(1)} %dynamic-slice_divide_fusion, s32[32,512]{1,0:T(8,128)S(1)} %pad_add_fusion), kind=kOutput, calls=%fused_computation.29 | convolution fusion | flops 1343488000 | bytes 4816896 | tf_op jit(solution)/shard_map/dot_general | solution.py:34
  264.1 9.3 %all-to-all-done.4 = bf16[32,16,1024]{2,1,0:T(8,128)(2,1)} async-done(((bf16[32,16,1024]{2,1,0:T(8,128)(2,1)}), bf16[32,16,1024]{2,1,0:T(8,128)(2,1)}, u32[]{:S(2)}, u32[]{:S(2)}) %all-to-all-start.4) | async-done | bytes 1048608 | tf_op jit(solution)/shard_map/all_to_all | solution.py:30
  273.4 1.8 fusion.46
  277.5 3.1 %collective-permute-start.11 = (bf16[128,1024]{1,0:T(8,128)(2,1)S(1)}, bf16[128,1024]{1,0:T(8,128)(2,1)S(1)}, u32[]{:S(2)}, u32[]{:S(2)}) collective-permute-start(bf16[128,1024]{1,0:T(8,128)(2,1)S(1)} %get-tuple-element.32), channel_id=1, source_target_pairs={{0,64},{32,96},{64,0},{96,32},{1,65},{33,97},{65,1},{97,33},{2,66}... | collective-permute-start | bytes 786440 | tf_op jit(solution)/shard_map/ppermute | solution.py:21
  280.6 10.2 %shard_map.121.refs_4_ = f32[704,1408]{1,0:T(8,128)} custom-call(bf16[704,768]{1,0:T(8,128)(2,1)} %copy-done.3, bf16[1408,768]{1,0:T(8,128)(2,1)} %pad_maximum_fusion.3.refs_1_), custom_call_target="tpu_custom_call" | custom-call | flops 1522532352 | bytes 7208960 | tf_op jit(solution)/shard_map/pallas_call | solution.py:254
  290.8 11.9 %shard_map.122 = f32[704,1408]{1,0:T(8,128)} custom-call(bf16[704,512]{1,0:T(8,128)(2,1)} %fusion.39.refs_0_, bf16[704,512]{1,0:T(8,128)(2,1)} %copy-done.5, bf16[1408,512]{1,0:T(8,128)(2,1)} %pad_maximum_fusion.4.refs_2_, bf16[1408,512]{1,0:T(8,128)(2,1)} %pad_maximum_fusion.5.refs_3_, f32[704,1408]{1,0:T(8,128)} %shard_map.121.refs_4_, ...), custom_call_target="tpu_custom_call" | custom-call | flops 2030043136 | bytes 8290304 | tf_op jit(solution)/shard_map/pallas_call | solution.py:254
  (133 shorter events, 23.0 us)
Async XLA Ops:
  0.6 157.4 %copy-start = (bf16[1,1,704,2048]{3,2,1,0:T(8,128)(2,1)S(1)}, bf16[1,1,704,2048]{3,2,1,0:T(8,128)(2,1)}, u32[]{:S(2)}) copy-start(bf16[1,1,704,2048]{3,2,1,0:T(8,128)(2,1)} %param.13) | copy-start | bytes 8650756
  0.6 20.3 %copy-start.18 = (s32[128,6]{0,1:T(8,128)S(1)}, s32[128,6]{0,1:T(8,128)}, u32[]{:S(2)}) copy-start(s32[128,6]{0,1:T(8,128)} %param.12) | copy-start | bytes 9220
  3.3 19.6 %collective-permute-start.4 = (bf16[128,2048]{1,0:T(8,128)(2,1)S(1)}, bf16[128,2048]{1,0:T(8,128)(2,1)}, u32[]{:S(2)}, u32[]{:S(2)}) collective-permute-start(bf16[128,2048]{1,0:T(8,128)(2,1)S(1)} %fusion.62), channel_id=1, source_target_pairs={{0,96},{32,64},{64,32},{96,0},{1,97},{33,65},{65,33},{97,1},{2,98}... | collective-permute-start | bytes 1572872 | tf_op jit(solution)/shard_map/ppermute | solution.py:21
  7.4 16.8 %collective-permute-start.3 = (bf16[128,2048]{1,0:T(8,128)(2,1)S(1)}, bf16[128,2048]{1,0:T(8,128)(2,1)}, u32[]{:S(2)}, u32[]{:S(2)}) collective-permute-start(bf16[128,2048]{1,0:T(8,128)(2,1)S(1)} %fusion.62), channel_id=1, source_target_pairs={{0,32},{32,0},{64,96},{96,64},{1,33},{33,1},{65,97},{97,65},{2,34}... | collective-permute-start | bytes 1572872 | tf_op jit(solution)/shard_map/ppermute | solution.py:21
  7.4 13.6 %collective-permute-start = (s32[6,128]{1,0:T(8,128)}, s32[6,128]{1,0:T(8,128)S(1)}, u32[]{:S(2)}, u32[]{:S(2)}) collective-permute-start(s32[6,128]{1,0:T(8,128)} %bitcast.132), channel_id=1, source_target_pairs={{0,32},{32,0},{64,96},{96,64},{1,33},{33,1},{65,97},{97,65},{2,34}... | collective-permute-start | bytes 9224 | tf_op jit(solution)/shard_map/ppermute | solution.py:21
  9.4 12.3 %collective-permute-start.1 = (s32[6,128]{1,0:T(8,128)}, s32[6,128]{1,0:T(8,128)S(1)}, u32[]{:S(2)}, u32[]{:S(2)}) collective-permute-start(s32[6,128]{1,0:T(8,128)} %bitcast.133), channel_id=1, source_target_pairs={{0,96},{32,64},{64,32},{96,0},{1,97},{33,65},{65,33},{97,1},{2,98}... | collective-permute-start | bytes 9224 | tf_op jit(solution)/shard_map/ppermute | solution.py:21
  9.5 12.3 %collective-permute-start.2 = (s32[6,128]{1,0:T(8,128)}, s32[6,128]{1,0:T(8,128)S(1)}, u32[]{:S(2)}, u32[]{:S(2)}) collective-permute-start(s32[6,128]{1,0:T(8,128)} %bitcast.134), channel_id=1, source_target_pairs={{0,64},{32,96},{64,0},{96,32},{1,65},{33,97},{65,1},{97,33},{2,66}... | collective-permute-start | bytes 9224 | tf_op jit(solution)/shard_map/ppermute | solution.py:21
  23.8 7.0 %collective-permute-start.5 = (bf16[64,2048]{1,0:T(8,128)(2,1)S(1)}, bf16[64,2048]{1,0:T(8,128)(2,1)S(1)}, u32[]{:S(2)}, u32[]{:S(2)}) collective-permute-start(bf16[64,2048]{1,0:T(8,128)(2,1)S(1)} %slice.47), channel_id=1, source_target_pairs={{0,32},{32,0},{64,96},{96,64},{1,33},{33,1},{65,97},{97,65},{2,34}... | collective-permute-start | bytes 786440 | tf_op jit(solution)/shard_map/ppermute | solution.py:21
  25.2 8.2 %collective-permute-start.6 = (bf16[64,2048]{1,0:T(8,128)(2,1)S(1)}, bf16[64,2048]{1,0:T(8,128)(2,1)S(1)}, u32[]{:S(2)}, u32[]{:S(2)}) collective-permute-start(bf16[64,2048]{1,0:T(8,128)(2,1)S(1)} %slice.48), channel_id=1, source_target_pairs={{0,96},{32,64},{64,32},{96,0},{1,97},{33,65},{65,33},{97,1},{2,98}... | collective-permute-start | bytes 786440 | tf_op jit(solution)/shard_map/ppermute | solution.py:21
  30.8 0.7 copy-start.14
  33.4 0.7 copy-start.15
  38.9 33.2 %all-to-all-start.1 = ((bf16[32,16,2048]{2,1,0:T(8,128)(2,1)}), bf16[32,16,2048]{2,1,0:T(8,128)(2,1)}, u32[]{:S(2)}, u32[]{:S(2)}) async-start(bf16[32,16,2048]{2,1,0:T(8,128)(2,1)} %bitcast.127), calls=%async_computation.1 | async-start | bytes 4194304 | tf_op jit(solution)/shard_map/all_to_all | solution.py:30
  47.6 0.8 copy-start.16
  72.1 36.2 %all-to-all-start.3 = ((bf16[32,16,2176]{2,1,0:T(8,128)(2,1)}), bf16[32,16,2176]{2,1,0:T(8,128)(2,1)}, u32[]{:S(2)}, u32[]{:S(2)}) async-start(bf16[32,16,2176]{2,1,0:T(8,128)(2,1)} %pad_maximum_fusion.2), calls=%async_computation.3 | async-start | bytes 4456448 | tf_op jit(solution)/shard_map/all_to_all | solution.py:30
  108.3 60.9 %all-to-all-start = ((bf16[32,24,2048]{2,1,0:T(8,128)(2,1)}), bf16[32,24,2048]{2,1,0:T(8,128)(2,1)}, u32[]{:S(2)}, u32[]{:S(2)}) async-start(bf16[32,24,2048]{2,1,0:T(8,128)(2,1)} %bitcast.121), calls=%async_computation | async-start | bytes 6291456 | tf_op jit(solution)/shard_map/all_to_all | solution.py:30
  117.6 2.9 copy-start.19
  117.6 2.9 copy-start.21
  117.6 2.9 copy-start.23
  117.6 2.9 copy-start.25
  117.6 3.0 copy-start.31
  120.3 33.9 %collective-permute-start.8 = (bf16[704,1024]{1,0:T(8,128)(2,1)}, bf16[704,1024]{1,0:T(8,128)(2,1)}, u32[]{:S(2)}, u32[]{:S(2)}) collective-permute-start(bf16[704,1024]{1,0:T(8,128)(2,1)} %dynamic-slice_bitcast_fusion), channel_id=1, source_target_pairs={{0,32},{32,0},{64,96},{96,64},{1,33},{33,1},{65,97},{97,65},{2,34}... | collective-permute-start | bytes 4325384 | tf_op jit(solution)/shard_map/ppermute | solution.py:21
  120.5 33.7 %copy-start.4 = (bf16[1,1,704,2048]{3,2,1,0:T(8,128)(2,1)S(1)}, bf16[1,1,704,2048]{3,2,1,0:T(8,128)(2,1)}, u32[]{:S(2)}) copy-start(bf16[1,1,704,2048]{3,2,1,0:T(8,128)(2,1)} %param.15) | copy-start | bytes 8650756
  158.0 3.4 %copy-start.28 = (bf16[1,1,704,2048]{3,2,1,0:T(8,128)(2,1)S(1)}, bf16[1,1,704,2048]{3,2,1,0:T(8,128)(2,1)}, u32[]{:S(2)}) copy-start(bf16[1,1,704,2048]{3,2,1,0:T(8,128)(2,1)} %param.14) | copy-start | bytes 8650756
  165.8 19.3 %collective-permute-start.9 = (bf16[704,512]{1,0:T(8,128)(2,1)}, bf16[704,512]{1,0:T(8,128)(2,1)}, u32[]{:S(2)}, u32[]{:S(2)}) collective-permute-start(bf16[704,512]{1,0:T(8,128)(2,1)} %fusion.39.refs_0_), channel_id=1, source_target_pairs={{0,32},{32,0},{64,96},{96,64},{1,33},{33,1},{65,97},{97,65},{2,34}... | collective-permute-start | bytes 2162696 | tf_op jit(solution)/shard_map/ppermute | solution.py:21
  169.2 4.5 %copy-start.29 = (bf16[1,1,704,2048]{3,2,1,0:T(8,128)(2,1)S(1)}, bf16[1,1,704,2048]{3,2,1,0:T(8,128)(2,1)}, u32[]{:S(2)}) copy-start(bf16[1,1,704,2048]{3,2,1,0:T(8,128)(2,1)} %param.14) | copy-start | bytes 8650756
  173.7 6.8 %copy-start.8 = (bf16[32,16,2048]{2,1,0:T(8,128)(2,1)S(1)}, bf16[32,16,2048]{2,1,0:T(8,128)(2,1)}, u32[]{:S(2)}) copy-start(bf16[32,16,2048]{2,1,0:T(8,128)(2,1)} %slice.52) | copy-start | bytes 6291460
  178.4 28.0 %copy-start.3 = (bf16[704,768]{1,0:T(8,128)(2,1)}, bf16[704,768]{1,0:T(8,128)(2,1)S(1)}, u32[]{:S(2)}) copy-start(bf16[704,768]{1,0:T(8,128)(2,1)S(1)} %fusion.12.refs_0_) | copy-start | bytes 3244036
  178.5 28.0 %collective-permute-start.7 = (bf16[704,768]{1,0:T(8,128)(2,1)S(1)}, bf16[704,768]{1,0:T(8,128)(2,1)S(1)}, u32[]{:S(2)}, u32[]{:S(2)}) collective-permute-start(bf16[704,768]{1,0:T(8,128)(2,1)S(1)} %fusion.12.refs_0_), channel_id=1, source_target_pairs={{0,32},{32,0},{64,96},{96,64},{1,33},{33,1},{65,97},{97,65},{2,34}... | collective-permute-start | bytes 3244040 | tf_op jit(solution)/shard_map/ppermute | solution.py:21
  183.3 3.2 %copy-start.9 = (bf16[704,1024]{1,0:T(8,128)(2,1)S(1)}, bf16[704,1024]{1,0:T(8,128)(2,1)}, u32[]{:S(2)}) copy-start(bf16[704,1024]{1,0:T(8,128)(2,1)} %get-tuple-element.22) | copy-start | bytes 4325380
  183.3 3.2 %copy-start.11 = (bf16[704,1024]{1,0:T(8,128)(2,1)S(1)}, bf16[704,1024]{1,0:T(8,128)(2,1)}, u32[]{:S(2)}) copy-start(bf16[704,1024]{1,0:T(8,128)(2,1)} %get-tuple-element.23) | copy-start | bytes 4325380
  186.5 1.9 copy-start.6
  186.5 1.9 copy-start.7
  211.0 40.0 %all-to-all-start.2 = ((bf16[32,40,1024]{2,1,0:T(8,128)(2,1)}), bf16[32,40,1024]{2,1,0:T(8,128)(2,1)}, u32[]{:S(2)}, u32[]{:S(2)}) async-start(bf16[32,40,1024]{2,1,0:T(8,128)(2,1)} %pad_maximum_fusion.1), calls=%async_computation.2 | async-start | bytes 5242880 | tf_op jit(solution)/shard_map/all_to_all | solution.py:30
  223.1 21.6 %copy-start.5 = (bf16[704,512]{1,0:T(8,128)(2,1)}, bf16[704,512]{1,0:T(8,128)(2,1)S(1)}, u32[]{:S(2)}) copy-start(bf16[704,512]{1,0:T(8,128)(2,1)S(1)} %fusion.36.refs_1_) | copy-start | bytes 2162692
  223.2 21.5 %collective-permute-start.10 = (bf16[704,512]{1,0:T(8,128)(2,1)S(1)}, bf16[704,512]{1,0:T(8,128)(2,1)}, u32[]{:S(2)}, u32[]{:S(2)}) collective-permute-start(bf16[704,512]{1,0:T(8,128)(2,1)S(1)} %fusion.36.refs_1_), channel_id=1, source_target_pairs={{0,32},{32,0},{64,96},{96,64},{1,33},{33,1},{65,97},{97,65},{2,34}... | collective-permute-start | bytes 2162696 | tf_op jit(solution)/shard_map/ppermute | solution.py:21
  245.9 1.9 copy-start.10
  245.9 2.3 copy-start.12
  251.0 22.4 %all-to-all-start.4 = ((bf16[32,16,1024]{2,1,0:T(8,128)(2,1)}), bf16[32,16,1024]{2,1,0:T(8,128)(2,1)}, u32[]{:S(2)}, u32[]{:S(2)}) async-start(bf16[32,16,1024]{2,1,0:T(8,128)(2,1)} %bitcast.131), calls=%async_computation.4 | async-start | bytes 2097152 | tf_op jit(solution)/shard_map/all_to_all | solution.py:30
  260.8 12.6 %copy-start.17 = (s32[32,256]{1,0:T(8,128)S(1)}, s32[32,256]{1,0:T(8,128)}, u32[]{:S(2)}) copy-start(s32[32,256]{1,0:T(8,128)} %copy-done.16) | copy-start | bytes 98308
  260.8 12.6 %copy-start.27 = (s32[16]{0:T(128)S(1)}, s32[16]{0:T(128)}, u32[]{:S(2)}) copy-start(s32[16]{0:T(128)} %copy-done.26) | copy-start | bytes 196
  275.9 26.8 %collective-permute-start.13 = (bf16[128,1024]{1,0:T(8,128)(2,1)}, bf16[128,1024]{1,0:T(8,128)(2,1)S(1)}, u32[]{:S(2)}, u32[]{:S(2)}) collective-permute-start(bf16[128,1024]{1,0:T(8,128)(2,1)} %get-tuple-element.33), channel_id=1, source_target_pairs={{0,96},{32,64},{64,32},{96,0},{1,97},{33,65},{65,33},{97,1},{2,98}... | collective-permute-start | bytes 786440 | tf_op jit(solution)/shard_map/ppermute | solution.py:21
  277.2 25.6 %collective-permute-start.12 = (bf16[128,1024]{1,0:T(8,128)(2,1)S(1)}, bf16[128,1024]{1,0:T(8,128)(2,1)S(1)}, u32[]{:S(2)}, u32[]{:S(2)}) collective-permute-start(bf16[128,1024]{1,0:T(8,128)(2,1)S(1)} %slice.68), channel_id=1, source_target_pairs={{0,32},{32,0},{64,96},{96,64},{1,33},{33,1},{65,97},{97,65},{2,34}... | collective-permute-start | bytes 786440 | tf_op jit(solution)/shard_map/ppermute | solution.py:21
  277.5 25.3 %collective-permute-start.11 = (bf16[128,1024]{1,0:T(8,128)(2,1)S(1)}, bf16[128,1024]{1,0:T(8,128)(2,1)S(1)}, u32[]{:S(2)}, u32[]{:S(2)}) collective-permute-start(bf16[128,1024]{1,0:T(8,128)(2,1)S(1)} %get-tuple-element.32), channel_id=1, source_target_pairs={{0,64},{32,96},{64,0},{96,32},{1,65},{33,97},{65,1},{97,33},{2,66}... | collective-permute-start | bytes 786440 | tf_op jit(solution)/shard_map/ppermute | solution.py:21
  302.8 1.0 copy-start.2
  302.8 1.8 copy-start.30
  302.8 1.8 copy-start.32
  303.0 2.7 copy-start.1
  304.1 1.6 copy-start.13
  (4 other events, 2.3 us)
where the time goes:
time: 311 us; the launch traced here: 306 us
  waiting for transfers between devices  113 us (36%)
  starting transfers between devices  59.4 us (19%)
  matrix products  51 us (16%)
  Pallas kernels  38.6 us (12%)
  other arithmetic  21.4 us (7%)
  local copies, waits for them, and re-layouts  20.5 us (7%)
    ppermute x14, waiting for transfers between devices, swapped(): return lax.ppermute(value, 'segment', pairs)  60.5 us
    all_to_all x5, waiting for transfers between devices, exchanged(): return lax.all_to_all(value, 'exp', split_axis=0, concat_axis=0, tiled=True)  52.4 us
    dot_general x19, matrix products, dot(): lax.dot_general(left, right, (dims, ((), ())), preferred_element_type=F32)  49.8 us
    all_to_all x5, starting transfers between devices, exchanged(): return lax.all_to_all(value, 'exp', split_axis=0, concat_axis=0, tiled=True)  41.5 us
    pallas_call x2, Pallas kernels, hidden_gram(): pl.pallas_call(functools.partial(hidden_gram_kernel, len(own)), grid=(wid...  22.1 us
    ppermute x14, starting transfers between devices, swapped(): return lax.ppermute(value, 'segment', pairs)  17.9 us
    pallas_call x1, Pallas kernels, scaled_gram(): pl.pallas_call(gram_kernel, grid_spec=pltpu.PrefetchScalarGridSpec(num_sc...  16.4 us
    unnamed x70, local copies, waits for them, and re-layouts  10.4 us
  transfers between devices with their start and end apart: 19, of which 9 were waited for; matrix products, arithmetic and copies ran while one was open for 23% of the time, Pallas kernels for 13%

commit v1 on v0

--- a/solution.py
+++ b/solution.py
@@ -150,19 +150,27 @@
         outs.append(out.reshape(columns, -1, width_half))
 
     mixes = []
-    for group, slot, part in ((RETURNS[0], slot_all, share), (RETURNS[1], slot_far, share[:, 2 * rows :])):
+    for number, (group, slot, part) in enumerate(
+        ((RETURNS[0], slot_all, share), (RETURNS[1], slot_far, share[:, 2 * rows :]))
+    ):
         low, size = lows[group[0]], sum(SIZES[i] for i in group)
         sent = jnp.concatenate([outs[i] for i in group], axis=1)
         back = exchanged(sent)
         back = back.reshape(columns * size, width_half)
         table = jnp.where(hits(slot, low, size), part[:, None, :], 0.0)
         table = table.reshape(columns * size, slot.shape[1])
-        mixes.append(dot(table.astype(BF16), back, ((0,), (0,))))
+        table = table.astype(BF16)
+        if number == 0:
+            mixes.append(dot(table, back, ((0,), (0,))))
+            continue
+        mixes.append(dot(table[:, rows:], back, ((0,), (0,))))
+        mixes.append(dot(table[:, :rows], back, ((0,), (0,))))
     mix_own = mixes[0][:rows]
     mix_mate = mixes[0][rows : 2 * rows]
-    mix_far = mixes[0][2 * rows :] + mixes[1]
-    from_far = swapped(mix_far[rows:].astype(BF16), FAR)
-    from_outer = swapped(mix_far[:rows].astype(BF16), OUTER)
+    mix_outer = mixes[0][2 * rows : 3 * rows] + mixes[2]
+    mix_far = mixes[0][3 * rows :] + mixes[1]
+    from_far = swapped(mix_far.astype(BF16), FAR)
+    from_outer = swapped(mix_outer.astype(BF16), OUTER)
     from_mate = swapped(mix_mate.astype(BF16), MATE)
     mine = mix_own + from_far.astype(F32)
     others = from_mate.astype(F32) + from_outer.astype(F32)
@@ -226,36 +234,48 @@
     )(half.astype(jnp.int32).reshape(1), scale.reshape(1, 1), *chunks, *chunks)
 
 
-def hidden_gram_kernel(count, *refs):
-    own, full = refs[:count], refs[count : 2 * count]
-    total = None
-    for a_ref, b_ref in zip(own, full):
-        part = dot(a_ref[...], b_ref[...], ((1,), (1,)))
-        total = part if total is None else total + part
-    if len(refs) > 2 * count + 1:
-        base_ref, scale_ref = refs[2 * count : 2 * count + 2]
-        total = (total + base_ref[...]) * scale_ref[0, 0]
-    refs[-1][...] = total
+def hidden_gram_kernel(count, wide, *refs):
+    own, full, out_ref = refs[:count], refs[count : 2 * count], refs[-1]
+    width = full[0].shape[0]
+    steps, step = width // wide, pl.program_id(0)
+
+    def columns(start, size):
+        total = None
+        for a_ref, b_ref in zip(own, full):
+            part = dot(a_ref[...], b_ref[pl.ds(start, size), :], ((1,), (1,)))
+            total = part if total is None else total + part
+        if len(refs) > 2 * count + 1:
+            base_ref, scale_ref = refs[2 * count : 2 * count + 2]
+            total = (total + base_ref[:, pl.ds(start, size)]) * scale_ref[0, 0]
+        out_ref[:, pl.ds(start, size)] = total
+
+    @pl.when(step < steps)
+    def _():
+        columns(pl.multiple_of(step * wide, wide), wide)
+
+    @pl.when(step == steps)
+    def _():
+        columns(steps * wide, width % wide)
 
 
 def hidden_gram(own, full, base=None, scale=None):
     units, width = own[0].shape[0], full[0].shape[0]
-    tile = 128
+    wide = 256
     depth = sum(v.shape[1] for v in own)
-    out_spec = pl.BlockSpec((units, tile), lambda j: (0, j))
+
+    def whole(shape):
+        return pl.BlockSpec(shape, lambda j: (0, 0), pipeline_mode=pl.Buffered(1))
+
     operands = (*own, *full)
-    specs = [
-        *[pl.BlockSpec((units, v.shape[1]), lambda j: (0, 0)) for v in own],
-        *[pl.BlockSpec((tile, v.shape[1]), lambda j: (j, 0)) for v in full],
-    ]
+    specs = [whole(v.shape) for v in operands]
     if base is not None:
         operands += (base, scale.reshape(1, 1))
-        specs += [out_spec, pl.BlockSpec(memory_space=pltpu.SMEM)]
+        specs += [whole(base.shape), pl.BlockSpec(memory_space=pltpu.SMEM)]
     return pl.pallas_call(
-        functools.partial(hidden_gram_kernel, len(own)),
-        grid=(width // tile,),
+        functools.partial(hidden_gram_kernel, len(own), wide),
+        grid=(width // wide + 1,),
         in_specs=specs,
-        out_specs=out_spec,
+        out_specs=pl.BlockSpec((units, width), lambda j: (0, 0)),
         out_shape=jax.ShapeDtypeStruct((units, width), F32),
         cost_estimate=pl.CostEstimate(
             flops=2 * depth * units * width,

time: 311 us -> 305 us (0.981)
  Pallas kernels: 38.6 us -> 32.1 us
  waiting for transfers between devices: 113 us -> 108 us
  other arithmetic: 21.4 us -> 25.9 us
    pallas_call x2, Pallas kernels: 22.1 us -> 15.7 us  [hidden_gram(): pl.pallas_call(functools.partial(hidden_gram_kernel, len(own), wide), gri...]
    all_to_all x5, waiting for transfers between devices: 52.4 us -> 47.8 us  [exchanged(): return lax.all_to_all(value, 'exp', split_axis=0, concat_axis=0, tiled=True)]
    dot_general x19 -> x20, matrix products: 49.8 us -> 50.9 us  [dot(): lax.dot_general(left, right, (dims, ((), ())), preferred_element_type=F32)]
    unnamed x70 -> x72, local copies, waits for them, and re-layouts: 10.4 us -> 10.4 us
  transfers between devices with their start and end apart: 19 -> 19, of which waited for: 9 -> 10; matrix products, arithmetic and copies ran while one was open for 23% -> 25% of each run, Pallas kernels for 13% -> 11%
where the time goes in v1:
time: 305 us; the launch traced here: 300 us
  waiting for transfers between devices  108 us (35%)
  starting transfers between devices  58.8 us (19%)
  matrix products  52.1 us (17%)
  Pallas kernels  32.1 us (11%)
  other arithmetic  25.9 us (8%)
  local copies, waits for them, and re-layouts  20.4 us (7%)
    ppermute x14, waiting for transfers between devices, swapped(): return lax.ppermute(value, 'segment', pairs)  60.5 us
    dot_general x20, matrix products, dot(): lax.dot_general(left, right, (dims, ((), ())), preferred_element_type=F32)  50.9 us
    all_to_all x5, waiting for transfers between devices, exchanged(): return lax.all_to_all(value, 'exp', split_axis=0, concat_axis=0, tiled=True)  47.8 us
    all_to_all x5, starting transfers between devices, exchanged(): return lax.all_to_all(value, 'exp', split_axis=0, concat_axis=0, tiled=True)  40.8 us
    ppermute x14, starting transfers between devices, swapped(): return lax.ppermute(value, 'segment', pairs)  18 us
    pallas_call x1, Pallas kernels, scaled_gram(): pl.pallas_call(gram_kernel, grid_spec=pltpu.PrefetchScalarGridSpec(num_sc...  16.4 us
    pallas_call x2, Pallas kernels, hidden_gram(): pl.pallas_call(functools.partial(hidden_gram_kernel, len(own), wide), gri...  15.7 us
    unnamed x72, local copies, waits for them, and re-layouts  10.4 us
  transfers between devices with their start and end apart: 19, of which 10 were waited for; matrix products, arithmetic and copies ran while one was open for 25% of the time, Pallas kernels for 11%

profile of v1, /device:TPU:26, one launch (start us, length us, event | category | flops | bytes accessed | tf_op | source)
XLA Modules:
  0.0 299.5 jit_solution(4355412279272259300)
XLA Ops:
  0.7 1.4 fusion.60
  3.3 4.1 %collective-permute-start.4 = (bf16[128,2048]{1,0:T(8,128)(2,1)S(1)}, bf16[128,2048]{1,0:T(8,128)(2,1)}, u32[]{:S(2)}, u32[]{:S(2)}) collective-permute-start(bf16[128,2048]{1,0:T(8,128)(2,1)S(1)} %fusion.62), channel_id=1, source_target_pairs={{0,96},{32,64},{64,32},{96,0},{1,97},{33,65},{65,33},{97,1},{2,98}... | collective-permute-start | bytes 1572872 | tf_op jit(solution)/shard_map/ppermute | solution.py:21
  7.4 2.0 collective-permute-start
  9.5 2.0 collective-permute-start.2
  12.5 8.5 %collective-permute-done = s32[6,128]{1,0:T(8,128)S(1)} collective-permute-done((s32[6,128]{1,0:T(8,128)}, s32[6,128]{1,0:T(8,128)S(1)}, u32[]{:S(2)}, u32[]{:S(2)}) %collective-permute-start) | collective-permute-done | bytes 3104 | tf_op jit(solution)/shard_map/ppermute | solution.py:21
  25.2 1.6 collective-permute-start.6
  26.8 1.9 constant_dynamic-update-slice_fusion.3
  28.7 1.9 constant_dynamic-update-slice_fusion.2
  34.8 4.2 %convolution_convert_fusion.2 = bf16[512,2048]{1,0:T(8,128)(2,1)} fusion(pred[512,512]{1,0:T(32,128)(4,1)S(1)} %bitcast_compare_fusion, bf16[512,2048]{1,0:T(8,128)(2,1)} %constant_dynamic-update-slice_fusion), kind=kOutput, calls=%fused_computation.2 | convolution fusion | flops 1074790400 | bytes 4456448 | tf_op jit(solution)/shard_map/dot_general | solution.py:34
  39.0 7.4 %all-to-all-start.1 = ((bf16[32,16,2048]{2,1,0:T(8,128)(2,1)}), bf16[32,16,2048]{2,1,0:T(8,128)(2,1)}, u32[]{:S(2)}, u32[]{:S(2)}) async-start(bf16[32,16,2048]{2,1,0:T(8,128)(2,1)} %bitcast.131), calls=%async_computation.1 | async-start | bytes 4194304 | tf_op jit(solution)/shard_map/all_to_all | solution.py:30
  49.4 1.9 convolution_convert_fusion.1
  51.5 1.5 pad_maximum_fusion.2
  53.0 19.1 %all-to-all-done.1 = bf16[32,16,2048]{2,1,0:T(8,128)(2,1)} async-done(((bf16[32,16,2048]{2,1,0:T(8,128)(2,1)}), bf16[32,16,2048]{2,1,0:T(8,128)(2,1)}, u32[]{:S(2)}, u32[]{:S(2)}) %all-to-all-start.1) | async-done | bytes 2097184 | tf_op jit(solution)/shard_map/all_to_all | solution.py:30
  72.1 9.1 %all-to-all-start.3 = ((bf16[32,16,2176]{2,1,0:T(8,128)(2,1)}), bf16[32,16,2176]{2,1,0:T(8,128)(2,1)}, u32[]{:S(2)}, u32[]{:S(2)}) async-start(bf16[32,16,2176]{2,1,0:T(8,128)(2,1)} %pad_maximum_fusion.2), calls=%async_computation.3 | async-start | bytes 4456448 | tf_op jit(solution)/shard_map/all_to_all | solution.py:30
  82.8 3.7 %convolution_convert_fusion = bf16[768,2048]{1,0:T(8,128)(2,1)} fusion(pred[768,256]{1,0:T(32,128)(4,1)S(1)} %bitcast_compare_fusion.1, bf16[128,2048]{1,0:T(8,128)(2,1)} %collective-permute-done.3, bf16[128,2048]{1,0:T(8,128)(2,1)S(1)} %fusion.62), kind=kOutput, calls=%fused_computation | convolution fusion | flops 808976384 | bytes 4390912 | tf_op jit(solution)/shard_map/dot_general | solution.py:34
  86.5 21.9 %all-to-all-done.3 = bf16[32,16,2176]{2,1,0:T(8,128)(2,1)} async-done(((bf16[32,16,2176]{2,1,0:T(8,128)(2,1)}), bf16[32,16,2176]{2,1,0:T(8,128)(2,1)}, u32[]{:S(2)}, u32[]{:S(2)}) %all-to-all-start.3) | async-done | bytes 2228256 | tf_op jit(solution)/shard_map/all_to_all | solution.py:30
  108.3 9.3 %all-to-all-start = ((bf16[32,24,2048]{2,1,0:T(8,128)(2,1)}), bf16[32,24,2048]{2,1,0:T(8,128)(2,1)}, u32[]{:S(2)}, u32[]{:S(2)}) async-start(bf16[32,24,2048]{2,1,0:T(8,128)(2,1)} %bitcast.123), calls=%async_computation | async-start | bytes 6291456 | tf_op jit(solution)/shard_map/all_to_all | solution.py:30
  117.7 2.6 dynamic-slice_bitcast_fusion
  120.7 2.5 fusion.89
  123.4 30.8 %collective-permute-done.8 = bf16[704,1024]{1,0:T(8,128)(2,1)} collective-permute-done((bf16[704,1024]{1,0:T(8,128)(2,1)}, bf16[704,1024]{1,0:T(8,128)(2,1)}, u32[]{:S(2)}, u32[]{:S(2)}) %collective-permute-start.8) | collective-permute-done | bytes 1441824 | tf_op jit(solution)/shard_map/ppermute | solution.py:21
  154.2 3.8 %bitcast_select_fusion.1 = (bf16[704,1024]{1,0:T(8,128)(2,1)}, bf16[704,1024]{1,0:T(8,128)(2,1)}) fusion(bf16[704,1024]{1,0:T(8,128)(2,1)} %collective-permute-done.8, pred[]{:T(512)S(6)} %eq.178, bf16[1,1,704,2048]{3,2,1,0:T(8,128)(2,1)S(1)} %copy-done.5, s32[]{:T(128)S(6)} %select_n.169), kind=kLoop, calls=%fused_computation.44 | loop fusion | flops 1441792 | bytes 5767173 | tf_op jit(solution)/shard_map/jit(_where)/select_n | solution.py:83
  158.0 3.4 %fusion.18 = f32[704,512]{1,0:T(8,128)S(1)} fusion(bf16[512,2048]{1,0:T(8,128)(2,1)} %bitcast.14.refs_1_.refs_4_, bf16[1,1,704,2048]{3,2,1,0:T(8,128)(2,1)S(1)} %copy-done), kind=kOutput, calls=%fused_computation.35 | convolution fusion | flops 1476395008 | bytes 6422528 | tf_op jit(solution)/shard_map/dot_general | solution.py:34
  161.4 4.3 %fusion.39.refs_0_ = bf16[704,512]{1,0:T(8,128)(2,1)} fusion(bf16[512,2048]{1,0:T(8,128)(2,1)} %bitcast.14.refs_1_.refs_4_, bf16[1,1,704,2048]{3,2,1,0:T(8,128)(2,1)S(1)} %copy-done.29, f32[704,512]{1,0:T(8,128)S(1)} %fusion.18), kind=kOutput, calls=%fused_computation.47 | convolution fusion | flops 1478557696 | bytes 7143424 | tf_op jit(solution)/shard_map/dot_general | solution.py:34
  166.1 3.2 %slice.55 = bf16[32,16,2048]{2,1,0:T(8,128)(2,1)} slice(bf16[32,16,2176]{2,1,0:T(8,128)(2,1)} %all-to-all-done.3), slice={[0:32], [0:16], [0:2048]} | slice | bytes 4194304 | tf_op jit(solution)/shard_map/slice | solution.py:134
  169.2 4.5 %fusion.10 = f32[768,704]{0,1:T(8,128)S(1)} fusion(bf16[768,2048]{1,0:T(8,128)(2,1)} %bitcast.4.refs_0_.refs_3_, bf16[1,1,704,2048]{3,2,1,0:T(8,128)(2,1)S(1)} %copy-done), kind=kOutput, calls=%fused_computation.14 | convolution fusion | flops 2214592512 | bytes 8192000 | tf_op jit(solution)/shard_map/dot_general | solution.py:34
  173.7 4.7 %fusion.12.refs_0_ = bf16[704,768]{1,0:T(8,128)(2,1)S(1)} fusion(f32[768,704]{0,1:T(8,128)S(1)} %fusion.10, bf16[768,2048]{1,0:T(8,128)(2,1)} %bitcast.4.refs_0_.refs_3_, bf16[1,1,704,2048]{3,2,1,0:T(8,128)(2,1)S(1)} %copy-done.30), kind=kOutput, calls=%fused_computation.22 | convolution fusion | flops 2217836544 | bytes 9273344 | tf_op jit(solution)/shard_map/dot_general | solution.py:34
  178.5 2.0 collective-permute-start.7
  180.5 2.8 fusion.21
  183.3 1.8 collective-permute-done.9
  185.1 1.4 broadcast_select_fusion.5
  186.6 1.8 convolution_convert_fusion.5
  188.4 18.1 %collective-permute-done.7 = bf16[704,768]{1,0:T(8,128)(2,1)S(1)} collective-permute-done((bf16[704,768]{1,0:T(8,128)(2,1)S(1)}, bf16[704,768]{1,0:T(8,128)(2,1)S(1)}, u32[]{:S(2)}, u32[]{:S(2)}) %collective-permute-start.7) | collective-permute-done | bytes 1081376 | tf_op jit(solution)/shard_map/ppermute | solution.py:21
  206.6 2.6 convolution_convert_fusion.3
  209.3 1.8 pad_maximum_fusion.1
  211.1 7.4 %all-to-all-start.2 = ((bf16[32,40,1024]{2,1,0:T(8,128)(2,1)}), bf16[32,40,1024]{2,1,0:T(8,128)(2,1)}, u32[]{:S(2)}, u32[]{:S(2)}) async-start(bf16[32,40,1024]{2,1,0:T(8,128)(2,1)} %pad_maximum_fusion.1), calls=%async_computation.2 | async-start | bytes 5242880 | tf_op jit(solution)/shard_map/all_to_all | solution.py:30
  218.5 4.7 %fusion.36.refs_1_ = bf16[704,512]{1,0:T(8,128)(2,1)S(1)} fusion(bf16[512,2048]{1,0:T(8,128)(2,1)} %bitcast.127, bf16[1,1,704,2048]{3,2,1,0:T(8,128)(2,1)} %param.14, f32[704,512]{1,0:T(8,128)} %fusion.21), kind=kOutput, calls=%fused_computation.46 | convolution fusion | flops 1478557696 | bytes 7143424 | tf_op jit(solution)/shard_map/dot_general | solution.py:34
  223.7 1.5 fusion.82
  225.9 2.3 pad_maximum_fusion.4.refs_2_
  228.2 16.4 %shard_map.120 = f32[1024,2048]{1,0:T(8,128)} custom-call(s32[1]{0:T(128)} %bitcast.27.half_ref, f32[1,1]{1,0:T(1,128)} %bitcast.28.scale_ref.refs_5_, bf16[768,2048]{1,0:T(8,128)(2,1)} %bitcast.4.refs_0_.refs_3_, bf16[512,2048]{1,0:T(8,128)(2,1)} %bitcast.14.refs_1_.refs_4_, bf16[512,2048]{1,0:T(8,128)(2,1)} %bitcast.128, ...), custom_call_target="tpu_custom_call" | custom-call | flops 7516192768 | bytes 30408704 | tf_op jit(solution)/shard_map/pallas_call | solution.py:219
  248.1 2.8 convolution_convert_fusion.4
  251.1 7.6 %all-to-all-start.4 = ((bf16[32,16,1024]{2,1,0:T(8,128)(2,1)}), bf16[32,16,1024]{2,1,0:T(8,128)(2,1)S(1)}, u32[]{:S(2)}, u32[]{:S(2)}) async-start(bf16[32,16,1024]{2,1,0:T(8,128)(2,1)} %bitcast.135), calls=%async_computation.4 | async-start | bytes 2097152 | tf_op jit(solution)/shard_map/all_to_all | solution.py:30
  258.7 2.7 pad_maximum_fusion.3.refs_1_
  261.4 3.3 %convolution_bitcast_fusion = f32[512,1024]{1,0:T(8,128)S(1)} fusion(bf16[32,40,1024]{2,1,0:T(8,128)(2,1)} %all-to-all-done.2, bf16[32,512]{1,0:T(8,128)(2,1)S(1)} %dynamic-slice_divide_fusion, s32[32,512]{1,0:T(8,128)S(1)} %pad_add_fusion), kind=kOutput, calls=%fused_computation.29 | convolution fusion | flops 1343488000 | bytes 4816896 | tf_op jit(solution)/shard_map/dot_general | solution.py:34
  266.1 6.7 %all-to-all-done.4 = bf16[32,16,1024]{2,1,0:T(8,128)(2,1)S(1)} async-done(((bf16[32,16,1024]{2,1,0:T(8,128)(2,1)}), bf16[32,16,1024]{2,1,0:T(8,128)(2,1)S(1)}, u32[]{:S(2)}, u32[]{:S(2)}) %all-to-all-start.4) | async-done | bytes 1048608 | tf_op jit(solution)/shard_map/all_to_all | solution.py:30
  274.1 1.4 fusion.45
  277.6 2.7 collective-permute-start.11
  280.3 6.8 %shard_map.121.refs_4_ = f32[704,1408]{1,0:T(8,128)} custom-call(bf16[704,768]{1,0:T(8,128)(2,1)} %copy-done.3, bf16[1408,768]{1,0:T(8,128)(2,1)} %pad_maximum_fusion.3.refs_1_), custom_call_target="tpu_custom_call" | custom-call | flops 1522532352 | bytes 7208960 | tf_op jit(solution)/shard_map/pallas_call | solution.py:274
  287.1 8.9 %shard_map.122 = f32[704,1408]{1,0:T(8,128)} custom-call(bf16[704,512]{1,0:T(8,128)(2,1)} %fusion.39.refs_0_, bf16[704,512]{1,0:T(8,128)(2,1)} %copy-done.6, bf16[1408,512]{1,0:T(8,128)(2,1)} %pad_maximum_fusion.4.refs_2_, bf16[1408,512]{1,0:T(8,128)(2,1)} %pad_maximum_fusion.5.refs_3_, f32[704,1408]{1,0:T(8,128)} %shard_map.121.refs_4_, ...), custom_call_target="tpu_custom_call" | custom-call | flops 2030043136 | bytes 8290304 | tf_op jit(solution)/shard_map/pallas_call | solution.py:274
  (136 shorter events, 28.7 us)
Async XLA Ops:
  0.6 157.4 %copy-start = (bf16[1,1,704,2048]{3,2,1,0:T(8,128)(2,1)S(1)}, bf16[1,1,704,2048]{3,2,1,0:T(8,128)(2,1)}, u32[]{:S(2)}) copy-start(bf16[1,1,704,2048]{3,2,1,0:T(8,128)(2,1)} %param.13) | copy-start | bytes 8650756
  0.6 20.3 %copy-start.21 = (s32[128,6]{0,1:T(8,128)S(1)}, s32[128,6]{0,1:T(8,128)}, u32[]{:S(2)}) copy-start(s32[128,6]{0,1:T(8,128)} %param.12) | copy-start | bytes 9220
  3.3 19.6 %collective-permute-start.4 = (bf16[128,2048]{1,0:T(8,128)(2,1)S(1)}, bf16[128,2048]{1,0:T(8,128)(2,1)}, u32[]{:S(2)}, u32[]{:S(2)}) collective-permute-start(bf16[128,2048]{1,0:T(8,128)(2,1)S(1)} %fusion.62), channel_id=1, source_target_pairs={{0,96},{32,64},{64,32},{96,0},{1,97},{33,65},{65,33},{97,1},{2,98}... | collective-permute-start | bytes 1572872 | tf_op jit(solution)/shard_map/ppermute | solution.py:21
  7.4 16.8 %collective-permute-start.3 = (bf16[128,2048]{1,0:T(8,128)(2,1)S(1)}, bf16[128,2048]{1,0:T(8,128)(2,1)}, u32[]{:S(2)}, u32[]{:S(2)}) collective-permute-start(bf16[128,2048]{1,0:T(8,128)(2,1)S(1)} %fusion.62), channel_id=1, source_target_pairs={{0,32},{32,0},{64,96},{96,64},{1,33},{33,1},{65,97},{97,65},{2,34}... | collective-permute-start | bytes 1572872 | tf_op jit(solution)/shard_map/ppermute | solution.py:21
  7.4 13.6 %collective-permute-start = (s32[6,128]{1,0:T(8,128)}, s32[6,128]{1,0:T(8,128)S(1)}, u32[]{:S(2)}, u32[]{:S(2)}) collective-permute-start(s32[6,128]{1,0:T(8,128)} %bitcast.136), channel_id=1, source_target_pairs={{0,32},{32,0},{64,96},{96,64},{1,33},{33,1},{65,97},{97,65},{2,34}... | collective-permute-start | bytes 9224 | tf_op jit(solution)/shard_map/ppermute | solution.py:21
  9.4 12.3 %collective-permute-start.1 = (s32[6,128]{1,0:T(8,128)}, s32[6,128]{1,0:T(8,128)S(1)}, u32[]{:S(2)}, u32[]{:S(2)}) collective-permute-start(s32[6,128]{1,0:T(8,128)} %bitcast.137), channel_id=1, source_target_pairs={{0,96},{32,64},{64,32},{96,0},{1,97},{33,65},{65,33},{97,1},{2,98}... | collective-permute-start | bytes 9224 | tf_op jit(solution)/shard_map/ppermute | solution.py:21
  9.5 12.3 %collective-permute-start.2 = (s32[6,128]{1,0:T(8,128)}, s32[6,128]{1,0:T(8,128)S(1)}, u32[]{:S(2)}, u32[]{:S(2)}) collective-permute-start(s32[6,128]{1,0:T(8,128)} %bitcast.138), channel_id=1, source_target_pairs={{0,64},{32,96},{64,0},{96,32},{1,65},{33,97},{65,1},{97,33},{2,66}... | collective-permute-start | bytes 9224 | tf_op jit(solution)/shard_map/ppermute | solution.py:21
  22.6 12.2 %copy-start.19 = (s32[32,128]{1,0:T(8,128)}, s32[32,128]{1,0:T(8,128)S(1)}, u32[]{:S(2)}) copy-start(s32[32,128]{1,0:T(8,128)S(1)} %fusion.55) | copy-start | bytes 49156
  23.8 7.0 %collective-permute-start.5 = (bf16[64,2048]{1,0:T(8,128)(2,1)S(1)}, bf16[64,2048]{1,0:T(8,128)(2,1)S(1)}, u32[]{:S(2)}, u32[]{:S(2)}) collective-permute-start(bf16[64,2048]{1,0:T(8,128)(2,1)S(1)} %slice.49), channel_id=1, source_target_pairs={{0,32},{32,0},{64,96},{96,64},{1,33},{33,1},{65,97},{97,65},{2,34}... | collective-permute-start | bytes 786440 | tf_op jit(solution)/shard_map/ppermute | solution.py:21
  25.2 8.2 %collective-permute-start.6 = (bf16[64,2048]{1,0:T(8,128)(2,1)S(1)}, bf16[64,2048]{1,0:T(8,128)(2,1)S(1)}, u32[]{:S(2)}, u32[]{:S(2)}) collective-permute-start(bf16[64,2048]{1,0:T(8,128)(2,1)S(1)} %slice.50), channel_id=1, source_target_pairs={{0,96},{32,64},{64,32},{96,0},{1,97},{33,65},{65,33},{97,1},{2,98}... | collective-permute-start | bytes 786440 | tf_op jit(solution)/shard_map/ppermute | solution.py:21
  39.0 33.2 %all-to-all-start.1 = ((bf16[32,16,2048]{2,1,0:T(8,128)(2,1)}), bf16[32,16,2048]{2,1,0:T(8,128)(2,1)}, u32[]{:S(2)}, u32[]{:S(2)}) async-start(bf16[32,16,2048]{2,1,0:T(8,128)(2,1)} %bitcast.131), calls=%async_computation.1 | async-start | bytes 4194304 | tf_op jit(solution)/shard_map/all_to_all | solution.py:30
  72.1 36.2 %all-to-all-start.3 = ((bf16[32,16,2176]{2,1,0:T(8,128)(2,1)}), bf16[32,16,2176]{2,1,0:T(8,128)(2,1)}, u32[]{:S(2)}, u32[]{:S(2)}) async-start(bf16[32,16,2176]{2,1,0:T(8,128)(2,1)} %pad_maximum_fusion.2), calls=%async_computation.3 | async-start | bytes 4456448 | tf_op jit(solution)/shard_map/all_to_all | solution.py:30
  108.3 60.9 %all-to-all-start = ((bf16[32,24,2048]{2,1,0:T(8,128)(2,1)}), bf16[32,24,2048]{2,1,0:T(8,128)(2,1)}, u32[]{:S(2)}, u32[]{:S(2)}) async-start(bf16[32,24,2048]{2,1,0:T(8,128)(2,1)} %bitcast.123), calls=%async_computation | async-start | bytes 6291456 | tf_op jit(solution)/shard_map/all_to_all | solution.py:30
  117.6 2.9 copy-start.22
  117.6 2.9 copy-start.24
  117.6 2.9 copy-start.26
  117.7 2.9 copy-start.28
  117.7 3.0 %copy-start.32 = (bf16[2048,64]{0,1:T(8,128)(2,1)S(1)}, bf16[2048,64]{0,1:T(8,128)(2,1)}, u32[]{:S(2)}) copy-start(bf16[2048,64]{0,1:T(8,128)(2,1)} %param.11) | copy-start | bytes 786436
  120.3 3.0 %copy-start.20 = (s32[512]{0:T(512)S(1)}, s32[512]{0:T(512)}, u32[]{:S(2)}) copy-start(s32[512]{0:T(512)} %eq.212) | copy-start | bytes 6148
  120.3 33.9 %collective-permute-start.8 = (bf16[704,1024]{1,0:T(8,128)(2,1)}, bf16[704,1024]{1,0:T(8,128)(2,1)}, u32[]{:S(2)}, u32[]{:S(2)}) collective-permute-start(bf16[704,1024]{1,0:T(8,128)(2,1)} %dynamic-slice_bitcast_fusion), channel_id=1, source_target_pairs={{0,32},{32,0},{64,96},{96,64},{1,33},{33,1},{65,97},{97,65},{2,34}... | collective-permute-start | bytes 4325384 | tf_op jit(solution)/shard_map/ppermute | solution.py:21
  120.6 33.7 %copy-start.5 = (bf16[1,1,704,2048]{3,2,1,0:T(8,128)(2,1)S(1)}, bf16[1,1,704,2048]{3,2,1,0:T(8,128)(2,1)}, u32[]{:S(2)}) copy-start(bf16[1,1,704,2048]{3,2,1,0:T(8,128)(2,1)} %param.15) | copy-start | bytes 8650756
  158.0 3.4 %copy-start.29 = (bf16[1,1,704,2048]{3,2,1,0:T(8,128)(2,1)S(1)}, bf16[1,1,704,2048]{3,2,1,0:T(8,128)(2,1)}, u32[]{:S(2)}) copy-start(bf16[1,1,704,2048]{3,2,1,0:T(8,128)(2,1)} %param.14) | copy-start | bytes 8650756
  165.8 19.3 %collective-permute-start.9 = (bf16[704,512]{1,0:T(8,128)(2,1)}, bf16[704,512]{1,0:T(8,128)(2,1)}, u32[]{:S(2)}, u32[]{:S(2)}) collective-permute-start(bf16[704,512]{1,0:T(8,128)(2,1)} %fusion.39.refs_0_), channel_id=1, source_target_pairs={{0,32},{32,0},{64,96},{96,64},{1,33},{33,1},{65,97},{97,65},{2,34}... | collective-permute-start | bytes 2162696 | tf_op jit(solution)/shard_map/ppermute | solution.py:21
  169.2 4.5 %copy-start.30 = (bf16[1,1,704,2048]{3,2,1,0:T(8,128)(2,1)S(1)}, bf16[1,1,704,2048]{3,2,1,0:T(8,128)(2,1)}, u32[]{:S(2)}) copy-start(bf16[1,1,704,2048]{3,2,1,0:T(8,128)(2,1)} %param.14) | copy-start | bytes 8650756
  173.7 6.8 %copy-start.10 = (bf16[32,16,2048]{2,1,0:T(8,128)(2,1)S(1)}, bf16[32,16,2048]{2,1,0:T(8,128)(2,1)}, u32[]{:S(2)}) copy-start(bf16[32,16,2048]{2,1,0:T(8,128)(2,1)} %slice.55) | copy-start | bytes 6291460
  178.5 28.0 %copy-start.3 = (bf16[704,768]{1,0:T(8,128)(2,1)}, bf16[704,768]{1,0:T(8,128)(2,1)S(1)}, u32[]{:S(2)}) copy-start(bf16[704,768]{1,0:T(8,128)(2,1)S(1)} %fusion.12.refs_0_) | copy-start | bytes 3244036
  178.5 28.0 %collective-permute-start.7 = (bf16[704,768]{1,0:T(8,128)(2,1)S(1)}, bf16[704,768]{1,0:T(8,128)(2,1)S(1)}, u32[]{:S(2)}, u32[]{:S(2)}) collective-permute-start(bf16[704,768]{1,0:T(8,128)(2,1)S(1)} %fusion.12.refs_0_), channel_id=1, source_target_pairs={{0,32},{32,0},{64,96},{96,64},{1,33},{33,1},{65,97},{97,65},{2,34}... | collective-permute-start | bytes 3244040 | tf_op jit(solution)/shard_map/ppermute | solution.py:21
  183.3 3.2 %copy-start.12 = (bf16[704,1024]{1,0:T(8,128)(2,1)S(1)}, bf16[704,1024]{1,0:T(8,128)(2,1)}, u32[]{:S(2)}) copy-start(bf16[704,1024]{1,0:T(8,128)(2,1)} %get-tuple-element.22) | copy-start | bytes 4325380
  183.3 3.3 %copy-start.14 = (bf16[704,1024]{1,0:T(8,128)(2,1)S(1)}, bf16[704,1024]{1,0:T(8,128)(2,1)}, u32[]{:S(2)}) copy-start(bf16[704,1024]{1,0:T(8,128)(2,1)} %get-tuple-element.23) | copy-start | bytes 4325380
  186.5 1.9 copy-start.7
  186.5 1.9 copy-start.9
  206.6 2.7 copy-start.4
  211.1 40.0 %all-to-all-start.2 = ((bf16[32,40,1024]{2,1,0:T(8,128)(2,1)}), bf16[32,40,1024]{2,1,0:T(8,128)(2,1)}, u32[]{:S(2)}, u32[]{:S(2)}) async-start(bf16[32,40,1024]{2,1,0:T(8,128)(2,1)} %pad_maximum_fusion.1), calls=%async_computation.2 | async-start | bytes 5242880 | tf_op jit(solution)/shard_map/all_to_all | solution.py:30
  218.5 7.3 %copy-start.8 = (bf16[704,512]{1,0:T(8,128)(2,1)S(1)}, bf16[704,512]{1,0:T(8,128)(2,1)}, u32[]{:S(2)}) copy-start(bf16[704,512]{1,0:T(8,128)(2,1)} %copy-done.7) | copy-start | bytes 2162692
  223.3 21.3 %copy-start.6 = (bf16[704,512]{1,0:T(8,128)(2,1)}, bf16[704,512]{1,0:T(8,128)(2,1)S(1)}, u32[]{:S(2)}) copy-start(bf16[704,512]{1,0:T(8,128)(2,1)S(1)} %fusion.36.refs_1_) | copy-start | bytes 2162692
  223.3 21.3 %collective-permute-start.10 = (bf16[704,512]{1,0:T(8,128)(2,1)S(1)}, bf16[704,512]{1,0:T(8,128)(2,1)}, u32[]{:S(2)}, u32[]{:S(2)}) collective-permute-start(bf16[704,512]{1,0:T(8,128)(2,1)S(1)} %fusion.36.refs_1_), channel_id=1, source_target_pairs={{0,32},{32,0},{64,96},{96,64},{1,33},{33,1},{65,97},{97,65},{2,34}... | collective-permute-start | bytes 2162696 | tf_op jit(solution)/shard_map/ppermute | solution.py:21
  245.8 1.9 copy-start.13
  245.8 2.3 copy-start.15
  251.1 21.7 %all-to-all-start.4 = ((bf16[32,16,1024]{2,1,0:T(8,128)(2,1)}), bf16[32,16,1024]{2,1,0:T(8,128)(2,1)S(1)}, u32[]{:S(2)}, u32[]{:S(2)}) async-start(bf16[32,16,1024]{2,1,0:T(8,128)(2,1)} %bitcast.135), calls=%async_computation.4 | async-start | bytes 2097152 | tf_op jit(solution)/shard_map/all_to_all | solution.py:30
  264.7 1.4 copy-start.11
  275.5 20.5 %collective-permute-start.13 = (bf16[128,1024]{1,0:T(8,128)(2,1)S(1)}, bf16[128,1024]{1,0:T(8,128)(2,1)S(1)}, u32[]{:S(2)}, u32[]{:S(2)}) collective-permute-start(bf16[128,1024]{1,0:T(8,128)(2,1)S(1)} %fusion.46), channel_id=1, source_target_pairs={{0,96},{32,64},{64,32},{96,0},{1,97},{33,65},{65,33},{97,1},{2,98}... | collective-permute-start | bytes 786440 | tf_op jit(solution)/shard_map/ppermute | solution.py:21
  276.9 19.1 %collective-permute-start.12 = (bf16[128,1024]{1,0:T(8,128)(2,1)S(1)}, bf16[128,1024]{1,0:T(8,128)(2,1)S(1)}, u32[]{:S(2)}, u32[]{:S(2)}) collective-permute-start(bf16[128,1024]{1,0:T(8,128)(2,1)S(1)} %slice.76), channel_id=1, source_target_pairs={{0,32},{32,0},{64,96},{96,64},{1,33},{33,1},{65,97},{97,65},{2,34}... | collective-permute-start | bytes 786440 | tf_op jit(solution)/shard_map/ppermute | solution.py:21
  277.6 18.4 %collective-permute-start.11 = (bf16[128,1024]{1,0:T(8,128)(2,1)S(1)}, bf16[128,1024]{1,0:T(8,128)(2,1)S(1)}, u32[]{:S(2)}, u32[]{:S(2)}) collective-permute-start(bf16[128,1024]{1,0:T(8,128)(2,1)S(1)} %fusion.45), channel_id=1, source_target_pairs={{0,64},{32,96},{64,0},{96,32},{1,65},{33,97},{65,1},{97,33},{2,66}... | collective-permute-start | bytes 786440 | tf_op jit(solution)/shard_map/ppermute | solution.py:21
  296.0 1.4 copy-start.2
  296.0 1.9 copy-start.31
  296.0 1.9 copy-start.33
  297.4 2.1 copy-start.1
  297.7 1.4 copy-start.16
  (5 other events, 3.2 us)
